TPU v7x, 32 devices: a whole 2x2x4 slice. The times are simulated.
32 devices in a mesh: tok: 16 (over z, y, core), tp: 2 (over x).
Axes of the slice: x: 2, y: 2, z: 4, core: 2. Of those that a mesh axis runs over, the one named last changes fastest.
Arguments:
- hidden_in: bfloat16 [4096, 4096], P('tok', 'tp'), may hold values from -6 to 6
- norm_gain: float32 [4096], replicated, may hold values from 0.5 to 9, as said below
- w_query: bfloat16 [4096, 4096], P(None, 'tp'), may hold values from -0.09375 to 0.09375
- w_key: bfloat16 [4096, 1024], P(None, 'tp'), may hold values from -0.09375 to 0.09375
- w_value: bfloat16 [4096, 1024], P(None, 'tp'), may hold values from -0.09375 to 0.09375
- w_out: bfloat16 [4096, 4096], P('tp'), may hold values from -0.5 to 0.5
- doc_ids: int32 [4096], replicated, may hold values from 0 to 3, never falling along the last dimension, each value on 1 to 3072 neighbouring positions
Outputs:
- hidden_out: bfloat16 [4096, 4096], P('tok', 'tp')
- joint_cov: float32 [2, 4096, 2, 4096], P(None, 'tok', None, 'tp')
Inputs may be any that keep to these rules, and one draw needn't show every extreme that they name: `norm_gain`: each channel's gain is positive. `doc_ids`: document numbers never fall along the tokens; a document holds 1 to 3072 tokens.
All inputs are finite; a program needn't handle non-finite values.
Results may differ from a plain program's by a relative error of at most 0.013.
The roundings to bfloat16 on the way count: a program that leaves them out, or rounds other values in their place, can miss the bound.
Values may be sent and summed in bfloat16 or wider, within the bound.
A program may use at most 192 MiB of HBM per device.

v0:
```python
import jax
import jax.numpy as jnp
from jax import lax
from jax.sharding import PartitionSpec as P

HS = 128
epsilon = 1e-05
rope_base = 500000.0


def broadcast(block, axis, source):
    block = jnp.where(lax.axis_index(axis) == source, block, jnp.zeros_like(block))
    return lax.psum(block, axis)


def rotate(vectors, positions):
    half_dim = vectors.shape[-1] // 2
    inv_freq = rope_base ** (-(jnp.arange(half_dim, dtype=jnp.float32) * 2.0) / vectors.shape[-1])
    angles = positions.astype(jnp.float32)[:, None] * inv_freq[None, :]
    cosine = jnp.cos(angles)[:, None, :]
    sine_part = jnp.sin(angles)[:, None, :]
    first_half = vectors[..., :half_dim]
    second_half = vectors[..., half_dim:]
    return jnp.concatenate(
        [
            first_half * cosine - second_half * sine_part,
            second_half * cosine + first_half * sine_part,
        ],
        axis=-1,
    )


def on_device(hidden_in, norm_gain, w_query, w_key, w_value, w_out, doc_ids):
    tok_rows = hidden_in.shape[0]
    col_width = hidden_in.shape[1]
    tok_count = lax.axis_size("tok")
    tok_index = lax.axis_index("tok")
    all_rows = tok_rows * tok_count
    full_in = lax.all_gather(hidden_in, "tp", axis=1, tiled=True)
    model_width = full_in.shape[1]
    row_width = model_width // tok_count
    widened = full_in.astype(jnp.float32)
    factor = lax.rsqrt(jnp.mean(widened * widened, axis=1, keepdims=True) + epsilon)
    normed = (widened * factor * norm_gain[None, :]).astype(jnp.bfloat16)
    kv_heads = w_key.shape[1] // HS
    groups = w_query.shape[1] // w_key.shape[1]
    first_row = tok_index * tok_rows
    positions = first_row + jnp.arange(tok_rows, dtype=jnp.int32)
    key_local = rotate(
        jnp.dot(normed, w_key, preferred_element_type=jnp.float32).reshape(tok_rows, kv_heads, HS),
        positions % all_rows,
    )
    key_local = key_local.astype(jnp.bfloat16).reshape(tok_rows, kv_heads * HS)
    value_local = jnp.dot(normed, w_value, preferred_element_type=jnp.float32).astype(jnp.bfloat16)
    key_rows, value_rows = (
        lax.all_gather(key_local, "tok", axis=0, tiled=True),
        lax.all_gather(value_local, "tok", axis=0, tiled=True),
    )
    queries = rotate(
        jnp.dot(normed, w_query, preferred_element_type=jnp.float32).reshape(
            tok_rows, kv_heads * groups, HS
        ),
        positions % all_rows,
    )
    queries = queries.astype(jnp.bfloat16).reshape(tok_rows, kv_heads, groups, HS)
    key_seq = key_rows.reshape(all_rows, kv_heads, HS)
    value_seq = value_rows.reshape(all_rows, kv_heads, HS)
    key_pos = jnp.arange(all_rows, dtype=jnp.int32)
    query_doc = lax.dynamic_slice_in_dim(doc_ids, first_row, tok_rows, 0)
    allowed = (query_doc[:, None] == doc_ids[None, :]) & (key_pos[None, :] <= positions[:, None])
    scores = jnp.einsum(
        "qhgd,khd->hgqk", queries, key_seq, preferred_element_type=jnp.float32
    ) * HS ** (-0.5)
    scores = jnp.where(allowed[None, None], scores, -jnp.inf)
    row_max = jnp.max(scores, axis=-1, keepdims=True)
    weights = jnp.exp(scores - row_max)
    weight_sum = jnp.sum(weights, axis=-1, keepdims=True)
    blended = (
        jnp.einsum(
            "hgqk,khd->hgqd",
            weights.astype(jnp.bfloat16),
            value_seq,
            preferred_element_type=jnp.float32,
        )
        / weight_sum
    )
    attended = (
        jnp.transpose(blended, (2, 0, 1, 3))
        .astype(jnp.bfloat16)
        .reshape(tok_rows, kv_heads * groups * HS)
    )
    partial_out = jnp.dot(attended, w_out, preferred_element_type=jnp.float32)
    summed = lax.psum_scatter(partial_out, "tp", scatter_dimension=1, tiled=True)
    hidden_out = (hidden_in.astype(jnp.float32) + summed).astype(jnp.bfloat16)
    columns = lax.all_gather(jnp.stack([hidden_in, hidden_out], axis=1), "tok", axis=0, tiled=True)
    offset = tok_index * row_width % col_width
    owner_rank = tok_index * row_width // col_width
    own_rows = lax.dynamic_slice_in_dim(columns, offset, row_width, 2)
    row_block = broadcast(own_rows, "tp", owner_rank).reshape(all_rows, 2 * row_width)
    flat_cols = columns.reshape(all_rows, 2 * col_width)
    gram_block = lax.dot_general(
        row_block, flat_cols, (((0,), (0,)), ((), ())), preferred_element_type=jnp.float32
    )
    col_sum = jnp.sum(flat_cols, axis=0, dtype=jnp.float32)
    row_mean = jnp.sum(row_block, axis=0, dtype=jnp.float32) / all_rows
    col_mean = col_sum / all_rows
    joint_cov = (gram_block / all_rows - row_mean[:, None] * col_mean[None, :]).reshape(
        2, row_width, 2, col_width
    )
    return (hidden_out, joint_cov)


def solution(mesh):
    return jax.shard_map(
        on_device,
        mesh=mesh,
        in_specs=(
            P("tok", "tp"),
            P(),
            P(None, "tp"),
            P(None, "tp"),
            P(None, "tp"),
            P("tp", None),
            P(),
        ),
        out_specs=(P("tok", "tp"), P(None, "tok", None, "tp")),
        check_vma=False,
    )
```

profile of v0, /device:TPU:0, one launch (start us, length us, event | category | flops | bytes accessed | tf_op | source)
XLA Modules:
  0.0 588.9 jit_solution(13531846354874264925)
XLA Ops:
  7.2 0.7 all-gather.5.cloned.1.call-update
  8.0 0.5 multiply_cosine_fusion
  8.5 36.8 %all-gather.5.cloned.1.call-done = bf16[256,4096]{1,0:T(8,128)(2,1)} async-done(((bf16[256,2048]{1,0:T(8,128)(2,1)}), bf16[256,4096]{1,0:T(8,128)(2,1)}) %all-gather.5.cloned.1.call-update) | async-done | bytes 2097168 | tf_op jit(solution)/shard_map/all_gather | solution.py:39
  45.4 2.1 fusion.6
  47.5 4.1 fusion.24
  51.8 0.5 subtract_convert_fusion.1
  52.7 0.9 copy.13
  53.7 1.9 fusion.9
  55.6 8.3 %convolution_bitcast_fusion = f32[32,8,16,128]{3,1,2,0:T(8,128)S(1)} fusion(bf16[4096,2048]{1,0:T(8,128)(2,1)} %param.9, bf16[256,4096]{1,0:T(8,128)(2,1)S(1)} %copy-done.2, f32[4096]{0:T(1024)S(1)} %copy-done.5, f32[256]{0:T(256)S(1)} %add_rsqrt_fusion), kind=kOutput, calls=%fused_computation.24 | convolution fusion | flops 4299161600 | bytes 20988928 | tf_op jit(solution)/shard_map/dot_general | solution.py:60
  63.9 0.4 copy.27
  64.3 0.8 subtract_convert_fusion
  65.1 1.2 copy.14
  66.3 1.2 copy.15
  67.5 2.0 convolution_convert_fusion
  69.8 36.4 %all-gather.7.cloned.1.call-done = bf16[4096,512]{0,1:T(8,128)(2,1)} async-done(((bf16[256,512]{0,1:T(8,128)(2,1)}), bf16[4096,512]{0,1:T(8,128)(2,1)}) %all-gather.7.cloned.1.call-update) | async-done | bytes 4194320 | tf_op jit(solution)/shard_map/all_gather | solution.py:56
  106.2 28.9 %fusion.2 = (f32[4,4,256]{2,1,0:T(4,128)S(1)}, f32[4,4096,256,4]{2,1,3,0:T(8,128)}) fusion(pred[256,4096]{0,1:T(8,128)(4,1)S(1)} %fusion.9, bf16[4096,4,128,1]{0,2,3,1:T(8,128)(2,1)} %bitcast.65, bf16[256,4,4,64]{3,0,2,1:T(8,128)(2,1)} %bitcast.60, bf16[256,4,4,64]{3,0,2,1:T(8,128)(2,1)} %bitcast.59), kind=kOutput, calls=%fused_computation.5 | convolution fusion | flops 4347392000 | bytes 73416704 | tf_op jit(solution)/shard_map/qhgd,khd->hgqk/dot_general | solution.py:71
  135.2 22.1 %fusion = f32[4,4,256]{2,1,0:T(4,128)S(1)} fusion(f32[4,4096,256,4]{2,1,3,0:T(8,128)} %get-tuple-element.9, f32[4,4,256]{2,1,0:T(4,128)S(1)} %get-tuple-element.8, pred[256,4096]{0,1:T(8,128)(4,1)S(1)} %fusion.9), kind=kLoop, calls=%fused_computation.3 | loop fusion | flops 67104768 | bytes 68190208 | tf_op jit(solution)/shard_map/reduce_sum | solution.py:77
  157.3 6.3 %copy.26 = bf16[4096,512]{0,1:T(8,128)(2,1)} copy(bf16[4096,512]{1,0:T(8,128)(2,1)} %all-gather.9.cloned.1.call-done) | data formatting | bytes 8388608 | tf_op jit(solution)/shard_map/reshape | solution.py:67
  163.6 25.5 %fusion.10 = bf16[256,4,4,128]{0,3,2,1:T(8,128)(2,1)S(1)} fusion(bf16[4096,4,128,1]{0,2,3,1:T(8,128)(2,1)} %bitcast.55, f32[4,4096,256,4]{2,1,3,0:T(8,128)} %get-tuple-element.9, f32[4,4,256]{2,1,0:T(4,128)S(1)} %get-tuple-element.8, pred[256,4096]{0,1:T(8,128)(4,1)S(1)} %fusion.9, f32[256,4,4]{0,2,1:T(4,128)S(1)} %bitcast.63), kind=kOutput, calls=%fused_computation.20 | convolution fusion | flops 4363124736 | bytes 73433088 | tf_op jit(solution)/shard_map/hgqk,khd->hgqd/dot_general | solution.py:79
  189.2 10.4 %fusion.26 = f32[256,4096]{1,0:T(8,128)} fusion(bf16[256,2048]{0,1:T(8,128)(2,1)S(1)} %bitcast.58, bf16[2048,4096]{1,0:T(8,128)(2,1)} %param.12), kind=kOutput, calls=%fused_computation.49 | convolution fusion | flops 4294967296 | bytes 22020096 | tf_op jit(solution)/shard_map/dot_general | solution.py:92
  199.7 52.7 %reduce-scatter.2.cloned.1.call-done = f32[256,2048]{1,0:T(8,128)} async-done(((f32[256,4096]{1,0:T(8,128)}), f32[256,2048]{1,0:T(8,128)}) %reduce-scatter.2.cloned.1.call-update) | async-done | bytes 2097168 | tf_op jit(solution)/shard_map/reduce_scatter | solution.py:93
  252.4 1.9 add_convert_fusion
  254.3 1.7 pad_maximum_fusion
  256.1 168.1 %all-gather.11.cloned.1.call-done = bf16[4096,2,2048]{2,0,1:T(8,128)(2,1)} async-done(((bf16[256,2,2048]{2,0,1:T(8,128)(2,1)}), bf16[4096,2,2048]{2,0,1:T(8,128)(2,1)}) %all-gather.11.cloned.1.call-update) | async-done | bytes 33554448 | tf_op jit(solution)/shard_map/all_gather | solution.py:95
  424.2 4.9 dynamic-slice_select_fusion
  429.2 12.4 %convert_reduce_fusion = f32[2,2048]{1,0:T(2,128)S(1)} fusion(bf16[4096,2,2048]{2,0,1:T(8,128)(2,1)} %all-gather.11.cloned.1.call-done), kind=kLoop, calls=%fused_computation.1 | loop fusion | flops 33550336 | bytes 33570816 | tf_op jit(solution)/shard_map/reduce_sum | solution.py:104
  441.6 40.5 %copy.20 = bf16[4096,2,2048]{0,2,1:T(8,128)(2,1)} copy(bf16[4096,2,2048]{2,0,1:T(8,128)(2,1)} %all-gather.11.cloned.1.call-done) | data formatting | bytes 67108864 | tf_op jit(solution)/shard_map/all_gather | solution.py:95
  482.0 55.2 %all-reduce.2.cloned.1.call-done = bf16[4096,2,256]{2,0,1:T(8,128)(2,1)} async-done(((bf16[4096,2,256]{2,0,1:T(8,128)(2,1)}), bf16[4096,2,256]{2,0,1:T(8,128)(2,1)}) %all-reduce.2.cloned.1.call-update) | async-done | bytes 4194320 | tf_op jit(solution)/shard_map/psum | solution.py:13
  537.2 2.8 convert_reduce_fusion.1
  540.0 6.3 %copy.19 = bf16[4096,2,256]{0,2,1:T(8,128)(2,1)} copy(bf16[4096,2,256]{2,0,1:T(8,128)(2,1)} %all-reduce.2.cloned.1.call-done) | data formatting | bytes 8388608 | tf_op jit(solution)/shard_map/psum | solution.py:13
  546.3 24.0 %multiply_subtract_fusion = f32[512,4096]{1,0:T(8,128)} fusion(bf16[4096,512]{0,1:T(8,128)(2,1)} %bitcast.56, bf16[4096,4096]{0,1:T(8,128)(2,1)} %bitcast.52, f32[4096]{0:T(1024)S(1)} %bitcast.62, f32[512]{0:T(512)S(1)} %bitcast.64), kind=kOutput, calls=%fused_computation.8 | convolution fusion | flops 17186160640 | bytes 46155776 | tf_op jit(solution)/shard_map/dot_general | solution.py:101
  570.4 11.7 %reshape.191 = f32[2,256,2,2048]{3,2,1,0:T(2,128)} reshape(f32[512,4096]{1,0:T(8,128)} %multiply_subtract_fusion) | data formatting | bytes 16777216 | tf_op jit(solution)/shard_map/reshape | solution.py:107
  (35 shorter events, 1.2 us)
Async XLA Ops:
  7.2 38.2 %all-gather.5.cloned.1.call-start = ((), (), s32[]{:S(2)}) async-start(), calls=%async_computation.1 | async-start | bytes 3145728 | tf_op jit(solution)/shard_map/all_gather | solution.py:39
  7.9 98.3 %all-gather.7.cloned.1.call-start = ((), (), s32[]{:S(2)}) async-start(), calls=%async_computation.2 | async-start | bytes 4456448 | tf_op jit(solution)/shard_map/all_gather | solution.py:56
  51.6 2.0 copy-start.3
  51.6 4.0 copy-start.2
  51.6 4.0 copy-start.5
  53.6 103.7 %all-gather.9.cloned.1.call-start = ((), (), s32[]{:S(2)}) async-start(), calls=%async_computation.3 | async-start | bytes 4456448 | tf_op jit(solution)/shard_map/all_gather | solution.py:57
  64.3 3.3 copy-start.4
  69.6 182.8 %reduce-scatter.2.cloned.1.call-start = ((), (), s32[]{:S(2)}) async-start(), calls=%async_computation.4 | async-start | bytes 6291456 | tf_op jit(solution)/shard_map/reduce_scatter | solution.py:93
  199.6 52.8 %copy-start = (bf16[256,2048]{1,0:T(8,128)(2,1)S(1)}, bf16[256,2048]{1,0:T(8,128)(2,1)}, u32[]{:S(2)}) copy-start(bf16[256,2048]{1,0:T(8,128)(2,1)} %param.7) | copy-start | bytes 3145732
  199.6 224.6 %all-gather.11.cloned.1.call-start = ((), (), s32[]{:S(2)}) async-start(), calls=%async_computation.5 | async-start | bytes 35651584 | tf_op jit(solution)/shard_map/all_gather | solution.py:95
  254.3 174.8 %copy-start.1 = (bf16[256,2048]{1,0:T(8,128)(2,1)}, bf16[256,2048]{1,0:T(8,128)(2,1)S(1)}, u32[]{:S(2)}) copy-start(bf16[256,2048]{1,0:T(8,128)(2,1)S(1)} %add_convert_fusion) | copy-start | bytes 3145732
  256.0 281.2 %all-reduce.2.cloned.1.call-start = ((), (), s32[]{:S(2)}) async-start(), calls=%async_computation.6 | async-start | bytes 8388608 | tf_op jit(solution)/shard_map/psum | solution.py:13
Sparse Core Ops, SparseCore 0:
  9.5 35.8 all-gather.4
  53.7 52.4 all-gather.6
  108.4 48.5 all-gather.8
  199.7 52.6 reduce-scatter.1
  256.1 168.0 all-gather.10
  429.3 107.8 all-reduce.1
where the time goes:
time: 591 us; the launch traced here: 589 us
  waiting for transfers between devices  350 us (59%)
  matrix products  103 us (17%)
  local copies, waits for them, and re-layouts  68.9 us (12%)
  other arithmetic  51.8 us (9%)
  between operations  14.4 us (2%)
    all_gather x1, waiting for transfers between devices, on_device(): lax.all_gather(jnp.stack([hidden_in, hidden_out], axis=1), 'tok', axis=0,...  168 us
    psum x1, waiting for transfers between devices, broadcast(): return lax.psum(block, axis)  55.2 us
    reduce_scatter x1, waiting for transfers between devices, on_device(): lax.psum_scatter(partial_out, 'tp', scatter_dimension=1, tiled=True)  52.7 us
    all_gather x1, local copies, waits for them, and re-layouts, on_device(): lax.all_gather(jnp.stack([hidden_in, hidden_out], axis=1), 'tok', axis=0,...  40.5 us
    all_gather x1, waiting for transfers between devices, on_device(): full_in = lax.all_gather(hidden_in, 'tp', axis=1, tiled=True)  36.8 us
    all_gather x1, waiting for transfers between devices, on_device(): lax.all_gather(key_local, 'tok', axis=0, tiled=True)  36.4 us
    dot_general x1, matrix products, on_device(): jnp.einsum('qhgd,khd->hgqk', queries, key_seq, preferred_element_type=jnp...  28.9 us
    dot_general x1, matrix products, on_device(): jnp.einsum('hgqk,khd->hgqd', weights.astype(jnp.bfloat16), value_seq, pre...  25.5 us
  transfers between devices with their start and end apart: 6, of which 5 were waited for; matrix products, arithmetic and copies ran while one was open for 20% of the time, Pallas kernels for 0%

commit v1 on v0

--- a/solution.py
+++ b/solution.py
@@ -36,7 +36,8 @@
     tok_count = lax.axis_size("tok")
     tok_index = lax.axis_index("tok")
     all_rows = tok_rows * tok_count
-    full_in = lax.all_gather(hidden_in, "tp", axis=1, tiled=True)
+    parts = lax.all_gather(hidden_in, "tp", axis=0, tiled=False)
+    full_in = jnp.concatenate(parts, axis=1)
     model_width = full_in.shape[1]
     row_width = model_width // tok_count
     widened = full_in.astype(jnp.float32)

time: 591 us -> 596 us (level)
  waiting for transfers between devices: 350 us -> 308 us
  local copies, waits for them, and re-layouts: 68.9 us -> 107 us
  other arithmetic: 51.8 us -> 61.2 us
    all_gather x1, waiting for transfers between devices: 36.4 us -> 0.02 us  [on_device(): lax.all_gather(key_local, 'tok', axis=0, tiled=True)]
    dot_general x0 -> x2, local copies, waits for them, and re-layouts: none -> 27.3 us  [the longest x1 20.9 us: on_device(): jnp.dot(normed, w_query, preferred_element_type=jnp.float32)]
    all_gather x1, waiting for transfers between devices: 36.8 us -> 30 us  [on_device(): parts = lax.all_gather(hidden_in, 'tp', axis=0, tiled=False)]
  transfers between devices with their start and end apart: 6 -> 6, of which waited for: 5 -> 5; matrix products, arithmetic and copies ran while one was open for 20% -> 27% of each run, Pallas kernels for 0% -> 0%
where the time goes in v1:
time: 596 us; the launch traced here: 593 us
  waiting for transfers between devices  308 us (52%)
  local copies, waits for them, and re-layouts  107 us (18%)
  matrix products  103 us (17%)
  other arithmetic  61.2 us (10%)
  between operations  14.3 us (2%)
    all_gather x1, waiting for transfers between devices, on_device(): lax.all_gather(jnp.stack([hidden_in, hidden_out], axis=1), 'tok', axis=0,...  168 us
    psum x1, waiting for transfers between devices, broadcast(): return lax.psum(block, axis)  54.6 us
    reduce_scatter x1, waiting for transfers between devices, on_device(): lax.psum_scatter(partial_out, 'tp', scatter_dimension=1, tiled=True)  53.2 us
    all_gather x1, local copies, waits for them, and re-layouts, on_device(): lax.all_gather(jnp.stack([hidden_in, hidden_out], axis=1), 'tok', axis=0,...  41 us
    all_gather x1, waiting for transfers between devices, on_device(): parts = lax.all_gather(hidden_in, 'tp', axis=0, tiled=False)  30 us
    dot_general x1, matrix products, on_device(): jnp.einsum('qhgd,khd->hgqk', queries, key_seq, preferred_element_type=jnp...  26.8 us
    dot_general x1, matrix products, on_device(): jnp.einsum('hgqk,khd->hgqd', weights.astype(jnp.bfloat16), value_seq, pre...  25.5 us
    dot_general x1, matrix products, on_device(): lax.dot_general(row_block, flat_cols, (((0,), (0,)), ((), ())), preferred...  24.1 us
  transfers between devices with their start and end apart: 6, of which 5 were waited for; matrix products, arithmetic and copies ran while one was open for 27% of the time, Pallas kernels for 0%

profile of v1, /device:TPU:0, one launch (start us, length us, event | category | flops | bytes accessed | tf_op | source)
XLA Modules:
  0.0 593.4 jit_solution(17636859583533429064)
XLA Ops:
  8.7 6.3 %copy.56 = bf16[512,4096]{1,0:T(8,128)(2,1)} copy(bf16[512,4096]{0,1:T(8,128)(2,1)} %bitcast.79) | data formatting | bytes 8388608 | tf_op jit(solution)/shard_map/dot_general | solution.py:51
  15.4 30.0 %all-gather.12.cloned.1.call-done = bf16[512,2048]{1,0:T(8,128)(2,1)} async-done(((bf16[256,2048]{1,0:T(8,128)(2,1)}), bf16[512,2048]{1,0:T(8,128)(2,1)}) %all-gather.12.cloned.1.call-update) | async-done | bytes 2097168 | tf_op jit(solution)/shard_map/all_gather | solution.py:39
  45.4 2.1 fusion.6
  47.5 2.2 fusion.12
  49.7 2.5 copy.37
  52.3 4.1 fusion.25
  57.2 20.9 %copy.60 = bf16[2048,4096]{1,0:T(8,128)(2,1)} copy(bf16[2048,4096]{0,1:T(8,128)(2,1)} %bitcast.76) | data formatting | bytes 33554432 | tf_op jit(solution)/shard_map/dot_general | solution.py:61
  78.2 1.9 fusion.11
  80.1 9.8 %fusion.26 = f32[256,16,128]{0,2,1:T(8,128)} fusion(bf16[256,4096,1]{0,1,2:T(8,128)(2,1)S(1)} %bitcast.87, bf16[16,128,4096]{2,1,0:T(8,128)(2,1)} %bitcast.77), kind=kOutput, calls=%fused_computation.53 | convolution fusion | flops 4294967296 | bytes 20971520 | tf_op jit(solution)/shard_map/dot_general | solution.py:61
  89.9 3.0 subtract_convert_fusion
  92.9 2.3 copy.42
  95.3 2.4 copy.43
  97.6 2.5 convert_bitcast_fusion
  100.2 5.4 copy.45
  105.5 2.7 fusion.10
  109.2 2.0 convolution_convert_fusion
  111.5 26.8 %fusion.2 = (f32[4,4,256]{2,1,0:T(4,128)S(1)}, f32[4,4096,256,4]{2,1,3,0:T(8,128)}) fusion(pred[256,4096]{0,1:T(8,128)(4,1)S(1)} %fusion.11, bf16[4096,4,128,1]{0,2,3,1:T(8,128)(2,1)} %bitcast.93, bf16[256,4,4,64]{3,0,2,1:T(8,128)(2,1)S(1)} %copy-done.5, bf16[256,4,4,64]{3,0,2,1:T(8,128)(2,1)S(1)} %copy-done.4), kind=kOutput, calls=%fused_computation.5 | convolution fusion | flops 4347392000 | bytes 73416704 | tf_op jit(solution)/shard_map/qhgd,khd->hgqk/dot_general | solution.py:72
  138.3 22.0 %fusion = f32[4,4,256]{2,1,0:T(4,128)S(1)} fusion(f32[4,4096,256,4]{2,1,3,0:T(8,128)} %get-tuple-element.9, f32[4,4,256]{2,1,0:T(4,128)S(1)} %get-tuple-element.8, pred[256,4096]{0,1:T(8,128)(4,1)S(1)} %fusion.11), kind=kLoop, calls=%fused_computation.3 | loop fusion | flops 67104768 | bytes 68190208 | tf_op jit(solution)/shard_map/reduce_sum | solution.py:78
  161.5 6.3 %copy.61 = bf16[4096,512]{0,1:T(8,128)(2,1)} copy(bf16[4096,512]{1,0:T(8,128)(2,1)} %all-gather.8.cloned.1.call-done) | data formatting | bytes 8388608 | tf_op jit(solution)/shard_map/reshape | solution.py:68
  167.8 25.5 %fusion.13 = bf16[256,4,4,128]{0,3,2,1:T(8,128)(2,1)S(1)} fusion(bf16[4096,4,128,1]{0,2,3,1:T(8,128)(2,1)} %bitcast.81, f32[4,4096,256,4]{2,1,3,0:T(8,128)} %get-tuple-element.9, f32[4,4,256]{2,1,0:T(4,128)S(1)} %get-tuple-element.8, pred[256,4096]{0,1:T(8,128)(4,1)S(1)} %fusion.11, f32[256,4,4]{0,2,1:T(4,128)S(1)} %bitcast.91), kind=kOutput, calls=%fused_computation.25 | convolution fusion | flops 4363124736 | bytes 73433088 | tf_op jit(solution)/shard_map/hgqk,khd->hgqd/dot_general | solution.py:80
  193.3 10.2 %fusion.27 = f32[256,4096]{1,0:T(8,128)} fusion(bf16[256,2048]{0,1:T(8,128)(2,1)S(1)} %bitcast.88, bf16[2048,4096]{1,0:T(8,128)(2,1)} %param.12), kind=kOutput, calls=%fused_computation.54 | convolution fusion | flops 4294967296 | bytes 22020096 | tf_op jit(solution)/shard_map/dot_general | solution.py:93
  203.6 53.2 %reduce-scatter.2.cloned.1.call-done = f32[256,2048]{1,0:T(8,128)} async-done(((f32[256,4096]{1,0:T(8,128)}), f32[256,2048]{1,0:T(8,128)}) %reduce-scatter.2.cloned.1.call-update) | async-done | bytes 2097168 | tf_op jit(solution)/shard_map/reduce_scatter | solution.py:94
  256.8 1.9 add_convert_fusion
  260.7 167.9 %all-gather.10.cloned.1.call-done = bf16[4096,2,2048]{2,0,1:T(8,128)(2,1)} async-done(((bf16[256,2,2048]{2,0,1:T(8,128)(2,1)}), bf16[4096,2,2048]{2,0,1:T(8,128)(2,1)}) %all-gather.10.cloned.1.call-update) | async-done | bytes 33554448 | tf_op jit(solution)/shard_map/all_gather | solution.py:96
  428.6 4.9 dynamic-slice_select_fusion
  433.5 12.4 %convert_reduce_fusion = f32[2,2048]{1,0:T(2,128)S(1)} fusion(bf16[4096,2,2048]{2,0,1:T(8,128)(2,1)} %all-gather.10.cloned.1.call-done), kind=kLoop, calls=%fused_computation.1 | loop fusion | flops 33550336 | bytes 33570816 | tf_op jit(solution)/shard_map/reduce_sum | solution.py:105
  445.9 41.0 %copy.49 = bf16[4096,2,2048]{0,2,1:T(8,128)(2,1)} copy(bf16[4096,2,2048]{2,0,1:T(8,128)(2,1)} %all-gather.10.cloned.1.call-done) | data formatting | bytes 67108864 | tf_op jit(solution)/shard_map/all_gather | solution.py:96
  487.0 54.6 %all-reduce.2.cloned.1.call-done = bf16[4096,2,256]{2,0,1:T(8,128)(2,1)} async-done(((bf16[4096,2,256]{2,0,1:T(8,128)(2,1)}), bf16[4096,2,256]{2,0,1:T(8,128)(2,1)}) %all-reduce.2.cloned.1.call-update) | async-done | bytes 4194320 | tf_op jit(solution)/shard_map/psum | solution.py:13
  541.6 2.8 convert_reduce_fusion.1
  544.4 6.3 %copy.48 = bf16[4096,2,256]{0,2,1:T(8,128)(2,1)} copy(bf16[4096,2,256]{2,0,1:T(8,128)(2,1)} %all-reduce.2.cloned.1.call-done) | data formatting | bytes 8388608 | tf_op jit(solution)/shard_map/psum | solution.py:13
  550.7 24.1 %multiply_subtract_fusion = f32[512,4096]{1,0:T(8,128)} fusion(bf16[4096,512]{0,1:T(8,128)(2,1)} %bitcast.82, bf16[4096,4096]{0,1:T(8,128)(2,1)} %bitcast.74, f32[4096]{0:T(1024)S(1)} %bitcast.90, f32[512]{0:T(512)S(1)} %bitcast.92), kind=kOutput, calls=%fused_computation.8 | convolution fusion | flops 17186160640 | bytes 46155776 | tf_op jit(solution)/shard_map/dot_general | solution.py:102
  574.8 11.7 %reshape.212 = f32[2,256,2,2048]{3,2,1,0:T(2,128)} reshape(f32[512,4096]{1,0:T(8,128)} %multiply_subtract_fusion) | data formatting | bytes 16777216 | tf_op jit(solution)/shard_map/reshape | solution.py:108
  (46 shorter events, 7.2 us)
Async XLA Ops:
  7.2 38.2 %all-gather.12.cloned.1.call-start = ((), (), s32[]{:S(2)}) async-start(), calls=%async_computation.6 | async-start | bytes 3145728 | tf_op jit(solution)/shard_map/all_gather | solution.py:39
  7.9 103.6 %all-gather.6.cloned.1.call-start = ((), (), s32[]{:S(2)}) async-start(), calls=%async_computation.1 | async-start | bytes 4456448 | tf_op jit(solution)/shard_map/all_gather | solution.py:57
  57.2 104.3 %all-gather.8.cloned.1.call-start = ((), (), s32[]{:S(2)}) async-start(), calls=%async_computation.2 | async-start | bytes 4456448 | tf_op jit(solution)/shard_map/all_gather | solution.py:58
  57.2 21.0 %copy-start.7 = (s32[4096]{0:T(1024)S(1)}, s32[4096]{0:T(1024)}, u32[]{:S(2)}) copy-start(s32[4096]{0:T(1024)} %param.13) | copy-start | bytes 49156
  57.2 22.9 %copy-start.3 = (bf16[256,2,2048]{0,2,1:T(8,128)(2,1)S(1)}, bf16[256,2,2048]{0,2,1:T(8,128)(2,1)}, u32[]{:S(2)}) copy-start(bf16[256,2,2048]{0,2,1:T(8,128)(2,1)} %copy.37) | copy-start | bytes 6291460
  89.9 7.7 %copy-start = (bf16[512,2048]{1,0:T(8,128)(2,1)S(1)}, bf16[512,2048]{1,0:T(8,128)(2,1)}, u32[]{:S(2)}) copy-start(bf16[512,2048]{1,0:T(8,128)(2,1)} %all-gather.12.cloned.1.call-done) | copy-start | bytes 6291460
  100.2 5.4 copy-start.6
  105.5 3.7 copy-start.8
  109.2 2.3 copy-start.4
  109.2 2.3 copy-start.5
  111.2 145.6 %reduce-scatter.2.cloned.1.call-start = ((), (), s32[]{:S(2)}) async-start(), calls=%async_computation.3 | async-start | bytes 6291456 | tf_op jit(solution)/shard_map/reduce_scatter | solution.py:94
  203.5 53.3 %copy-start.1 = (bf16[256,2048]{1,0:T(8,128)(2,1)S(1)}, bf16[256,2048]{1,0:T(8,128)(2,1)}, u32[]{:S(2)}) copy-start(bf16[256,2048]{1,0:T(8,128)(2,1)} %param.7) | copy-start | bytes 3145732
  203.5 225.0 %all-gather.10.cloned.1.call-start = ((), (), s32[]{:S(2)}) async-start(), calls=%async_computation.4 | async-start | bytes 35651584 | tf_op jit(solution)/shard_map/all_gather | solution.py:96
  258.7 174.8 %copy-start.2 = (bf16[256,2048]{1,0:T(8,128)(2,1)}, bf16[256,2048]{1,0:T(8,128)(2,1)S(1)}, u32[]{:S(2)}) copy-start(bf16[256,2048]{1,0:T(8,128)(2,1)S(1)} %add_convert_fusion) | copy-start | bytes 3145732
  260.4 281.2 %all-reduce.2.cloned.1.call-start = ((), (), s32[]{:S(2)}) async-start(), calls=%async_computation.5 | async-start | bytes 8388608 | tf_op jit(solution)/shard_map/psum | solution.py:13
Sparse Core Ops, SparseCore 0:
  9.5 35.8 all-gather.11
  57.3 52.4 all-gather.5
  112.5 48.8 all-gather.7
  203.7 53.0 reduce-scatter.1
  260.5 168.0 all-gather.9
  433.7 107.8 all-reduce.1
